TPU v7x, 32 devices: a whole 2x2x4 slice. The times are simulated.
32 devices in a mesh: row: 2 (over core), pitch: 4 (over y, x), span: 4 (over z).
Axes of the slice: x: 2, y: 2, z: 4, core: 2. Of those that a mesh axis runs over, the one named last changes fastest.
Arguments:
- snapshots: bfloat16 [2, 20, 3, 32, 256, 256], P('row', None, None, 'pitch', 'span'), may hold values from -6 to 6
- snap_index: int32 [16], replicated, may hold values from 0 to 19, as said below
- flow_state: float32 [2, 5, 32, 256, 256], P('row', None, 'pitch', 'span'), may hold values from -6 to 6
- eddy_viscosity: float32 [2, 32, 256, 256], P('row', 'pitch', 'span'), may hold values from 0.04 to 0.4
- intersection: int32 [2, 32], P('row'), may hold values from 0 to 31, as said below
- counts: int32 [2, 32], P('row'), may hold values from 1 to 8, as said below
Outputs:
- received_stress: float32 [2, 6, 256, 256], P('row', None, 'span')
- new_state: float32 [2, 5, 32, 256, 256], P('row', None, 'pitch', 'span')
Inputs may be any that keep to these rules, and one draw needn't show every extreme that they name: `snap_index`: 16 distinct slots, among them slot 0 and slot 19. `intersection`: for each row, a one-to-one map of blocks. Call blocks k * 8 to (k + 1) * 8 - 1 group k: the blocks of one group take their sources from at most 2 blocks of any one group of the other layout, and exactly 2 for some pairs of groups. `counts`: each row has a block with all 8 cells live.
All inputs are finite; a program needn't handle non-finite values.
Results may differ from a plain program's by a relative error of at most 0.0003.
Values sent between devices are 32-bit elements; how exact they have to be, the bound alone decides.
A program may use at most 128 MiB of HBM per device.

v0:
```python
import jax
import jax.numpy as jnp
from jax import lax
from jax.sharding import PartitionSpec as P

SNAPS = 16
BLOCK = 8
CAPACITY = 2
stress_pairs = ((0, 0), (0, 1), (0, 2), (1, 1), (1, 2), (2, 2))
time_step = 0.1


def padded_2(block, sides, width, periodic):
    for axis, dim in sides:
        count = lax.axis_size(axis)
        forward = [(i, i + 1) for i in range(count - 1)]
        if periodic:
            forward.append((count - 1, 0))
        backward = [(target, source) for source, target in forward]
        low = lax.ppermute(
            lax.slice_in_dim(block, block.shape[dim] - width, None, axis=dim), axis, forward
        )
        high = lax.ppermute(lax.slice_in_dim(block, 0, width, axis=dim), axis, backward)
        block = jnp.concatenate([low, block, high], axis=dim)
    return block


def partner(block, axis, bit):
    count = lax.axis_size(axis)
    route = []
    for low in range(count):
        high = low | 1 << bit
        if high != low and high < count:
            route += [(low, high), (high, low)]
    return lax.ppermute(block, axis, route)


def axial_diff(values):
    padded = jnp.concatenate([values[..., :1], values, values[..., -1:]], axis=-1)
    return (padded[..., 2:] - padded[..., :-2]) * 0.5


def residual(flow_field, speed, viscosity, live_mask, forcing):
    around_pitch = padded_2(flow_field, (("pitch", 1),), 1, True)
    around_span = padded_2(flow_field, (("span", 2),), 1, False)
    axial_pad = jnp.concatenate([flow_field[..., :1], flow_field, flow_field[..., -1:]], axis=3)
    laplace = (
        around_pitch[:, 2:]
        + around_pitch[:, :-2]
        + around_span[:, :, 2:]
        + around_span[:, :, :-2]
        + axial_pad[..., 2:]
        + axial_pad[..., :-2]
        - 6.0 * flow_field
    )
    return live_mask * (-axial_diff(speed * flow_field) + viscosity * laplace + forcing)


def deliver(values, block_links):
    swapped = partner(values, "row", 0)
    span_count = lax.axis_size("span")
    blocks_all = block_links.shape[0]
    per_dev = blocks_all // span_count
    share_len = swapped.shape[2]
    block_len = swapped.shape[1] // per_dev
    position = lax.axis_index("span")
    block_ids = jnp.arange(blocks_all, dtype=jnp.int32)
    pairing = (block_links[:, None] == block_ids[None, :]).astype(jnp.int32)
    target = jnp.sum(pairing * block_ids[:, None], axis=0)
    target_dev = target // per_dev
    source_dev = block_ids // per_dev
    earlier = (
        (source_dev[:, None] == source_dev[None, :])
        & (target_dev[:, None] == target_dev[None, :])
        & (block_ids[None, :] < block_ids[:, None])
    )
    slot_of = jnp.sum(earlier.astype(jnp.int32), axis=1)
    devices = jnp.arange(span_count, dtype=jnp.int32)
    places = jnp.arange(CAPACITY, dtype=jnp.int32)
    my_dev = lax.dynamic_slice_in_dim(target_dev, position * per_dev, per_dev)
    my_slot = lax.dynamic_slice_in_dim(slot_of, position * per_dev, per_dev)
    placing = (
        (my_dev[:, None, None] == devices[None, :, None])
        & (my_slot[:, None, None] == places[None, None, :])
    ).astype(jnp.float32)
    blocks = swapped.reshape(6, per_dev, block_len * share_len)
    outgoing = jnp.einsum("jnc,mjw->ncmw", placing, blocks, precision=lax.Precision.HIGHEST)
    incoming = lax.all_to_all(outgoing, "span", split_axis=0, concat_axis=0, tiled=True)
    wanted = lax.dynamic_slice_in_dim(block_links, position * per_dev, per_dev)
    from_dev = wanted // per_dev
    from_slot = jnp.sum(
        (wanted[:, None] == block_ids[None, :]).astype(jnp.int32) * slot_of[None, :], axis=1
    )
    choosing = (
        (from_dev[:, None, None] == devices[None, :, None])
        & (from_slot[:, None, None] == places[None, None, :])
    ).astype(jnp.float32)
    arrived = jnp.einsum("knc,ncmw->mkw", choosing, incoming, precision=lax.Precision.HIGHEST)
    return arrived.reshape(6, per_dev * block_len, share_len)


def body(snapshots, snap_index, flow_state, eddy_viscosity, intersection, counts):
    stored = snapshots[0]
    start = flow_state[0]
    viscosity = eddy_viscosity[0]
    block_links = intersection[0]
    block_counts = counts[0]
    pitch_cells = stored.shape[2]
    span_cells = stored.shape[3]
    axial_cells = stored.shape[4]
    pitch_total = pitch_cells * lax.axis_size("pitch")

    def select_slot(slot):
        return lax.dynamic_index_in_dim(stored, slot, 0, keepdims=False).astype(jnp.float32)

    def add_mean(step_num, running):
        return running + select_slot(snap_index[step_num])

    running = lax.fori_loop(0, SNAPS, add_mean, jnp.zeros(stored.shape[1:], jnp.float32))
    time_mean = running / SNAPS

    def add_products(step_num, running):
        fluct = select_slot(snap_index[step_num]) - time_mean
        return running + jnp.stack([jnp.sum(fluct[p] * fluct[q], axis=0) for p, q in stress_pairs])

    summed = lax.fori_loop(
        0, SNAPS, add_products, jnp.zeros((6, span_cells, axial_cells), jnp.float32)
    )
    partial_value = summed / (SNAPS * pitch_total)
    totals = lax.psum(partial_value, "pitch")
    received = deliver(totals, block_links)
    position = lax.axis_index("span")
    span_total = span_cells * lax.axis_size("span")
    span_pos = (
        (position * span_cells + jnp.arange(span_cells, dtype=jnp.int32)).astype(jnp.float32) + 0.5
    ) / span_total
    curvature = (1.0 / (1.0 + span_pos))[:, None]
    source_x = -axial_diff(received[0]) - curvature * received[1]
    source_r = -axial_diff(received[1]) + curvature * (received[5] - received[3])
    source_t = -axial_diff(received[2]) - 2.0 * curvature * received[4]
    energy = time_mean[0] * source_x + time_mean[1] * source_r + time_mean[2] * source_t
    forcing = jnp.concatenate(
        [
            jnp.zeros((1, pitch_cells, span_cells, axial_cells), jnp.float32),
            jnp.broadcast_to(
                jnp.stack([source_x, source_r, source_t])[:, None],
                (3, pitch_cells, span_cells, axial_cells),
            ),
            energy[None],
        ],
        axis=0,
    )
    per_dev = span_cells // BLOCK
    my_counts = lax.dynamic_slice_in_dim(block_counts, position * per_dev, per_dev)
    live_mask = (jnp.arange(BLOCK, dtype=jnp.int32)[None, :] < my_counts[:, None]).astype(
        jnp.float32
    )
    live_mask = live_mask.reshape(span_cells)[:, None]
    speed = 0.5 + time_mean[0]
    section_one = start + time_step * residual(start, speed, viscosity, live_mask, forcing)
    finished = 0.5 * (
        start
        + section_one
        + time_step * residual(section_one, speed, viscosity, live_mask, forcing)
    )
    return (received[None], finished[None])


def solution(mesh):
    return jax.shard_map(
        body,
        mesh=mesh,
        in_specs=(
            P("row", None, None, "pitch", "span", None),
            P(),
            P("row", None, "pitch", "span", None),
            P("row", "pitch", "span", None),
            P("row", None),
            P("row", None),
        ),
        out_specs=(P("row", None, "span", None), P("row", None, "pitch", "span", None)),
        check_vma=False,
    )
```

profile of v0, /device:TPU:0, one launch (start us, length us, event | category | flops | bytes accessed | tf_op | source)
XLA Modules:
  0.0 288.5 jit_solution(12164644477243232642)
XLA Ops:
  7.2 1.8 fusion.64
  10.3 6.2 %collective-permute-start.4 = (f32[5,8,1,256]{3,2,1,0:T(1,128)}, f32[5,8,1,256]{3,2,1,0:T(1,128)}, u32[]{:S(2)}, u32[]{:S(2)}) collective-permute-start(f32[5,8,1,256]{3,2,1,0:T(1,128)} %get-tuple-element.251), channel_id=1, source_target_pairs={{0,1},{1,2},{2,3},{4,5},{5,6},{6,7},{8,9},{9,10},{10,11},{12,13},{... | collective-permute-start | bytes 122888 | tf_op jit(solution)/shard_map/ppermute | solution.py:20
  16.5 2.0 fusion.63
  18.4 2.9 collective-permute-start.1
  21.3 77.6 %while.28 = (s32[]{:T(128)}, f32[3,8,64,256]{3,2,1,0:T(8,128)S(1)}, s32[16]{0:T(128)}, bf16[20,3,8,64,256]{4,3,2,1,0:T(8,128)(2,1)}, s32[]{:T(128)}, /*index=5*/s32[]{:T(128)}, s32[]{:T(128)}) while((s32[]{:T(128)}, f32[3,8,64,256]{3,2,1,0:T(8,128)S(1)}, s32[16]{0:T(128)}, bf16[20,3,8,64,256]{4,3,2,1,0:T(8,128)(2,1)}, s32[]{:T(128)}, ...), condition=%wide.region_3.0_spmd.clone, body=%wide.region_2.3_spmd.clone.sunk | while | flops 1179654 | bytes 3932305 | solution.py:119
  24.5 1.7 convert_add_fusion.2
  29.3 1.7 convert_add_fusion.2
  34.2 1.7 convert_add_fusion.2
  39.0 1.7 convert_add_fusion.2
  43.9 1.7 convert_add_fusion.2
  48.7 1.7 convert_add_fusion.2
  53.6 1.7 convert_add_fusion.2
  58.4 1.7 convert_add_fusion.2
  63.3 1.7 convert_add_fusion.2
  68.1 1.7 convert_add_fusion.2
  73.0 1.7 convert_add_fusion.2
  77.8 1.7 convert_add_fusion.2
  82.7 1.7 convert_add_fusion.2
  87.5 1.7 convert_add_fusion.2
  92.4 1.7 convert_add_fusion.2
  97.2 1.7 convert_add_fusion.2
  99.6 69.6 %while.29 = (s32[]{:T(128)}, f32[6,64,256]{2,1,0:T(8,128)S(1)}, s32[16]{0:T(128)S(1)}, bf16[20,3,8,64,256]{4,3,2,1,0:T(8,128)(2,1)}, f32[3,8,64,256]{3,2,1,0:T(8,128)S(1)}, /*index=5*/s32[]{:T(128)}, s32[]{:T(128)}, s32[]{:T(128)}) while((s32[]{:T(128)}, f32[6,64,256]{2,1,0:T(8,128)S(1)}, s32[16]{0:T(128)S(1)}, ...), condition=%wide.region_11.12_spmd.clone, body=%wide.region_4.11_spmd.clone.sunk | while | flops 2457606 | bytes 7864473 | solution.py:126
  102.1 1.4 convert_subtract_fusion.2
  106.4 1.4 convert_subtract_fusion.2
  110.8 1.4 convert_subtract_fusion.2
  115.1 1.4 convert_subtract_fusion.2
  119.5 1.4 convert_subtract_fusion.2
  123.8 1.4 convert_subtract_fusion.2
  128.2 1.4 convert_subtract_fusion.2
  132.5 1.4 convert_subtract_fusion.2
  136.9 1.4 convert_subtract_fusion.2
  141.2 1.4 convert_subtract_fusion.2
  145.6 1.4 convert_subtract_fusion.2
  149.9 1.4 convert_subtract_fusion.2
  170.7 44.2 %all-reduce.2.cloned.1.call-done = f32[6,64,256]{2,1,0:T(8,128)} async-done(((f32[6,64,256]{2,1,0:T(8,128)}), f32[6,64,256]{2,1,0:T(8,128)}) %all-reduce.2.cloned.1.call-update) | async-done | bytes 393232 | tf_op jit(solution)/shard_map/psum | solution.py:130
  215.0 1.9 collective-permute-done
  218.2 4.6 %all-to-all-start = ((f32[4,2,6,2048]{3,1,2,0:T(2,128)}), f32[4,2,6,2048]{3,1,2,0:T(2,128)S(1)}, u32[]{:S(2)}, u32[]{:S(2)}) async-start(f32[4,2,6,2048]{3,1,2,0:T(2,128)} %fusion.48), calls=%async_computation | async-start | bytes 786432 | tf_op jit(solution)/shard_map/all_to_all | solution.py:88
  222.9 3.2 %fusion.65 = (f32[5,8,64,1]{3,2,1,0:T(8,128)S(1)}, f32[5,8,64,1]{3,2,1,0:T(8,128)}) fusion(f32[5,8,64,256]{3,2,1,0:T(8,128)} %bitcast.77), kind=kLoop, calls=%fused_computation.139 | loop fusion | bytes 40960 | tf_op jit(solution)/shard_map/slice | solution.py:46
  226.1 8.6 %all-to-all-done = f32[4,2,6,2048]{3,1,2,0:T(2,128)S(1)} async-done(((f32[4,2,6,2048]{3,1,2,0:T(2,128)}), f32[4,2,6,2048]{3,1,2,0:T(2,128)S(1)}, u32[]{:S(2)}, u32[]{:S(2)}) %all-to-all-start) | async-done | bytes 393248 | tf_op jit(solution)/shard_map/all_to_all | solution.py:88
  238.3 2.0 fusion.62
  240.5 6.7 %broadcast_multiply_fusion = (f32[5,8,64,256]{3,2,1,0:T(8,128)S(1)}, f32[5,8,64,256]{3,2,1,0:T(8,128)S(1)}) fusion(f32[8,64,256]{2,1,0:T(8,128)S(1)} %get-tuple-element.255, f32[5,8,64,256]{3,2,1,0:T(8,128)S(1)} %bitcast.78, f32[1,8,64,256]{3,2,1,0:T(8,128)S(1)} %get-tuple-element.254, f32[3,8,64,256]{3,2,1,0:T(8,128)S(1)} %broadcast_in_dim.13, ...), kind=kLoop, calls=%fused_computation.65 | loop fusion | flops 17694720 | bytes 14410004 | tf_op jit(solution)/shard_map/mul | solution.py:56
  248.3 1.9 fusion.61
  250.2 1.5 collective-permute-start.5
  254.2 4.5 %collective-permute-start.8 = (f32[5,8,1,256]{3,2,1,0:T(1,128)S(1)}, f32[5,8,1,256]{3,2,1,0:T(1,128)S(1)}, u32[]{:S(2)}, u32[]{:S(2)}) collective-permute-start(f32[5,8,1,256]{3,2,1,0:T(1,128)S(1)} %get-tuple-element.243), channel_id=1, source_target_pairs={{0,1},{1,2},{2,3},{4,5},{5,6},{6,7},{8,9},{9,10},{10,11},{12,13},{... | collective-permute-start | bytes 122888 | tf_op jit(solution)/shard_map/ppermute | solution.py:20
  258.7 1.9 fusion.58
  260.7 1.8 broadcast_in_dim_reshape.3
  262.5 4.6 %collective-permute-done.6 = f32[5,1,64,256]{3,2,1,0:T(8,128)} collective-permute-done((f32[5,1,64,256]{3,2,1,0:T(8,128)}, f32[5,1,64,256]{3,2,1,0:T(8,128)}, u32[]{:S(2)}, u32[]{:S(2)}) %collective-permute-start.6) | collective-permute-done | bytes 327712 | tf_op jit(solution)/shard_map/ppermute | solution.py:20
  267.0 14.6 %fusion.9 = f32[1,5,8,64,256]{4,3,2,1,0:T(8,128)} fusion(f32[5,8,64,256]{3,2,1,0:T(8,128)} %copy-done.2, f32[5,8,64,1]{3,2,1,0:T(8,128)} %get-tuple-element.245, f32[5,8,64,1]{3,2,1,0:T(8,128)S(1)} %get-tuple-element.244, f32[5,8,1,256]{3,2,1,0:T(1,128)S(1)} %collective-permute-done.8, f32[5,8,1,256]{3,2,1,0:T(1,128)S(1)} %collective-permute-done.7, ...), kind=kLoop, calls=%fused_computation.25 | loop fusion | flops 18350080 | bytes 13885716 | tf_op jit(solution)/shard_map/broadcast_in_dim | solution.py:166
  (232 shorter events, 53.5 us)
Async XLA Ops:
  7.2 162.8 %copy-start = (s32[1,32]{1,0:T(1,128)S(1)}, s32[1,32]{1,0:T(1,128)}, u32[]{:S(2)}) copy-start(s32[1,32]{1,0:T(1,128)} %param.15) | copy-start | bytes 388
  7.2 207.7 %all-reduce.2.cloned.1.call-start = ((), (), s32[]{:S(2)}) async-start(), calls=%async_computation.1 | async-start | bytes 786432 | tf_op jit(solution)/shard_map/psum | solution.py:130
  9.0 231.3 %collective-permute-start.3 = (f32[5,8,1,256]{3,2,1,0:T(1,128)}, f32[5,8,1,256]{3,2,1,0:T(1,128)}, u32[]{:S(2)}, u32[]{:S(2)}) collective-permute-start(f32[5,8,1,256]{3,2,1,0:T(1,128)} %get-tuple-element.250), channel_id=1, source_target_pairs={{1,0},{2,1},{3,2},{5,4},{6,5},{7,6},{9,8},{10,9},{11,10},{13,12},{... | collective-permute-start | bytes 122888 | tf_op jit(solution)/shard_map/ppermute | solution.py:23
  10.3 230.1 %collective-permute-start.4 = (f32[5,8,1,256]{3,2,1,0:T(1,128)}, f32[5,8,1,256]{3,2,1,0:T(1,128)}, u32[]{:S(2)}, u32[]{:S(2)}) collective-permute-start(f32[5,8,1,256]{3,2,1,0:T(1,128)} %get-tuple-element.251), channel_id=1, source_target_pairs={{0,1},{1,2},{2,3},{4,5},{5,6},{6,7},{8,9},{9,10},{10,11},{12,13},{... | collective-permute-start | bytes 122888 | tf_op jit(solution)/shard_map/ppermute | solution.py:20
  18.4 221.9 %collective-permute-start.1 = (f32[5,1,64,256]{3,2,1,0:T(8,128)}, f32[5,1,64,256]{3,2,1,0:T(8,128)}, u32[]{:S(2)}, u32[]{:S(2)}) collective-permute-start(f32[5,1,64,256]{3,2,1,0:T(8,128)} %get-tuple-element.248), channel_id=1, source_target_pairs={{4,0},{8,4},{12,8},{0,12},{5,1},{9,5},{13,9},{1,13},{6,2},{10,6},{... | collective-permute-start | bytes 983048 | tf_op jit(solution)/shard_map/ppermute | solution.py:23
  21.3 219.0 %collective-permute-start.2 = (f32[5,1,64,256]{3,2,1,0:T(8,128)}, f32[5,1,64,256]{3,2,1,0:T(8,128)}, u32[]{:S(2)}, u32[]{:S(2)}) collective-permute-start(f32[5,1,64,256]{3,2,1,0:T(8,128)} %get-tuple-element.249), channel_id=1, source_target_pairs={{0,4},{4,8},{8,12},{12,0},{1,5},{5,9},{9,13},{13,1},{2,6},{6,10},{... | collective-permute-start | bytes 983048 | tf_op jit(solution)/shard_map/ppermute | solution.py:20
  98.9 0.7 copy-start.6
  99.5 70.5 %copy-start.5 = (s32[1,32]{1,0:T(1,128)S(1)}, s32[1,32]{1,0:T(1,128)}, u32[]{:S(2)}) copy-start(s32[1,32]{1,0:T(1,128)} %param.14) | copy-start | bytes 388
  214.9 1.9 collective-permute-start
  218.2 16.6 %all-to-all-start = ((f32[4,2,6,2048]{3,1,2,0:T(2,128)}), f32[4,2,6,2048]{3,1,2,0:T(2,128)S(1)}, u32[]{:S(2)}, u32[]{:S(2)}) async-start(f32[4,2,6,2048]{3,1,2,0:T(2,128)} %fusion.48), calls=%async_computation | async-start | bytes 786432 | tf_op jit(solution)/shard_map/all_to_all | solution.py:88
  235.3 0.8 copy-start.4
  236.3 1.7 copy-start.1
  247.3 4.9 %copy-start.2 = (f32[5,8,64,256]{3,2,1,0:T(8,128)}, f32[5,8,64,256]{3,2,1,0:T(8,128)S(1)}, u32[]{:S(2)}) copy-start(f32[5,8,64,256]{3,2,1,0:T(8,128)S(1)} %get-tuple-element.235) | copy-start | bytes 7864324
  247.3 11.5 %copy-start.3 = (f32[5,8,64,256]{3,2,1,0:T(8,128)}, f32[5,8,64,256]{3,2,1,0:T(8,128)S(1)}, u32[]{:S(2)}) copy-start(f32[5,8,64,256]{3,2,1,0:T(8,128)S(1)} %get-tuple-element.234) | copy-start | bytes 7864324
  250.2 12.3 %collective-permute-start.5 = (f32[5,1,64,256]{3,2,1,0:T(8,128)}, f32[5,1,64,256]{3,2,1,0:T(8,128)}, u32[]{:S(2)}, u32[]{:S(2)}) collective-permute-start(f32[5,1,64,256]{3,2,1,0:T(8,128)} %get-tuple-element.240), channel_id=1, source_target_pairs={{4,0},{8,4},{12,8},{0,12},{5,1},{9,5},{13,9},{1,13},{6,2},{10,6},{... | collective-permute-start | bytes 983048 | tf_op jit(solution)/shard_map/ppermute | solution.py:23
  251.6 15.4 %collective-permute-start.6 = (f32[5,1,64,256]{3,2,1,0:T(8,128)}, f32[5,1,64,256]{3,2,1,0:T(8,128)}, u32[]{:S(2)}, u32[]{:S(2)}) collective-permute-start(f32[5,1,64,256]{3,2,1,0:T(8,128)} %get-tuple-element.241), channel_id=1, source_target_pairs={{0,4},{4,8},{8,12},{12,0},{1,5},{5,9},{9,13},{13,1},{2,6},{6,10},{... | collective-permute-start | bytes 983048 | tf_op jit(solution)/shard_map/ppermute | solution.py:20
  252.9 9.6 %collective-permute-start.7 = (f32[5,8,1,256]{3,2,1,0:T(1,128)}, f32[5,8,1,256]{3,2,1,0:T(1,128)S(1)}, u32[]{:S(2)}, u32[]{:S(2)}) collective-permute-start(f32[5,8,1,256]{3,2,1,0:T(1,128)} %get-tuple-element.242), channel_id=1, source_target_pairs={{1,0},{2,1},{3,2},{5,4},{6,5},{7,6},{9,8},{10,9},{11,10},{13,12},{... | collective-permute-start | bytes 122888 | tf_op jit(solution)/shard_map/ppermute | solution.py:23
  254.2 8.3 %collective-permute-start.8 = (f32[5,8,1,256]{3,2,1,0:T(1,128)S(1)}, f32[5,8,1,256]{3,2,1,0:T(1,128)S(1)}, u32[]{:S(2)}, u32[]{:S(2)}) collective-permute-start(f32[5,8,1,256]{3,2,1,0:T(1,128)S(1)} %get-tuple-element.243), channel_id=1, source_target_pairs={{0,1},{1,2},{2,3},{4,5},{5,6},{6,7},{8,9},{9,10},{10,11},{12,13},{... | collective-permute-start | bytes 122888 | tf_op jit(solution)/shard_map/ppermute | solution.py:20
Sparse Core Ops, SparseCore 0:
  170.0 44.8 all-reduce.1
where the time goes:
time: 291 us; the launch traced here: 289 us
  other arithmetic  77.3 us (27%)
  loops' own time  63.3 us (22%)
  waiting for transfers between devices  59.3 us (20%)
  local copies, waits for them, and re-layouts  49.7 us (17%)
  starting transfers between devices  22.9 us (8%)
  between operations  14.3 us (5%)
    psum x1, waiting for transfers between devices, body(): totals = lax.psum(partial_value, 'pitch')  44.2 us
    another operation x1, loops' own time, body(): lax.fori_loop(0, SNAPS, add_products, jnp.zeros((6, span_cells, axial_cel...  32.4 us
    another operation x1, loops' own time, body(): lax.fori_loop(0, SNAPS, add_mean, jnp.zeros(stored.shape[1:], jnp.float32))  30.9 us
    add x16, other arithmetic, add_mean(): return running + select_slot(snap_index[step_num])  26.5 us
    sub x16, other arithmetic, add_products(): fluct = select_slot(snap_index[step_num]) - time_mean  21.6 us
    dynamic_slice x16, local copies, waits for them, and re-layouts, add_mean(): return running + select_slot(snap_index[step_num])  20.2 us
    broadcast_in_dim x1, other arithmetic, body(): return (received[None], finished[None])  14.6 us
    ppermute x4, starting transfers between devices, padded_2(): lax.ppermute(lax.slice_in_dim(block, block.shape[dim] - width, None, axis...  11.3 us
  transfers between devices with their start and end apart: 11, of which 4 were waited for; matrix products, arithmetic and copies ran while one was open for 35% of the time, Pallas kernels for 0%

commit v1 on v0

--- a/solution.py
+++ b/solution.py
@@ -2,6 +2,7 @@
 import jax.numpy as jnp
 from jax import lax
 from jax.sharding import PartitionSpec as P
+from jax.lax import all_gather
 
 SNAPS = 16
 BLOCK = 8
@@ -127,7 +128,11 @@
         0, SNAPS, add_products, jnp.zeros((6, span_cells, axial_cells), jnp.float32)
     )
     partial_value = summed / (SNAPS * pitch_total)
-    totals = lax.psum(partial_value, "pitch")
+
+    def pass_pieces_all(raw, a_name):
+        return jnp.sum(all_gather(raw, axis_name=a_name), axis=0)
+
+    totals = pass_pieces_all(partial_value, "pitch")
     received = deliver(totals, block_links)
     position = lax.axis_index("span")
     span_total = span_cells * lax.axis_size("span")

time: 291 us -> 276 us (0.948)
  waiting for transfers between devices: 59.3 us -> 42.1 us
    psum x1 -> x0, waiting for transfers between devices: 44.2 us -> none  [body(): totals = lax.psum(partial_value, 'pitch')]
    all_gather x0 -> x1, waiting for transfers between devices: none -> 26.6 us  [pass_pieces_all(): return jnp.sum(all_gather(raw, axis_name=a_name), axis=0)]
  transfers between devices with their start and end apart: 11 -> 11, of which waited for: 4 -> 4; matrix products, arithmetic and copies ran while one was open for 35% -> 7% of each run, Pallas kernels for 0% -> 0%
where the time goes in v1:
time: 276 us; the launch traced here: 273 us
  other arithmetic  79.5 us (29%)
  loops' own time  63.3 us (23%)
  local copies, waits for them, and re-layouts  49.7 us (18%)
  waiting for transfers between devices  42.1 us (15%)
  starting transfers between devices  21.9 us (8%)
  between operations  14.4 us (5%)
    another operation x1, loops' own time, body(): lax.fori_loop(0, SNAPS, add_products, jnp.zeros((6, span_cells, axial_cel...  32.4 us
    another operation x1, loops' own time, body(): lax.fori_loop(0, SNAPS, add_mean, jnp.zeros(stored.shape[1:], jnp.float32))  30.9 us
    all_gather x1, waiting for transfers between devices, pass_pieces_all(): return jnp.sum(all_gather(raw, axis_name=a_name), axis=0)  26.6 us
    add x16, other arithmetic, add_mean(): return running + select_slot(snap_index[step_num])  26.5 us
    sub x16, other arithmetic, add_products(): fluct = select_slot(snap_index[step_num]) - time_mean  21.6 us
    dynamic_slice x16, local copies, waits for them, and re-layouts, add_mean(): return running + select_slot(snap_index[step_num])  20.2 us
    broadcast_in_dim x1, other arithmetic, body(): return (received[None], finished[None])  14.8 us
    ppermute x4, starting transfers between devices, padded_2(): lax.ppermute(lax.slice_in_dim(block, block.shape[dim] - width, None, axis...  10.7 us
  transfers between devices with their start and end apart: 11, of which 4 were waited for; matrix products, arithmetic and copies ran while one was open for 7% of the time, Pallas kernels for 0%

profile of v1, /device:TPU:0, one launch (start us, length us, event | category | flops | bytes accessed | tf_op | source)
XLA Modules:
  0.0 272.7 jit_solution(1790245470005030771)
XLA Ops:
  7.2 77.6 %while.28 = (s32[]{:T(128)}, f32[3,8,64,256]{3,2,1,0:T(8,128)S(1)}, s32[16]{0:T(128)}, bf16[20,3,8,64,256]{4,3,2,1,0:T(8,128)(2,1)}, s32[]{:T(128)}, /*index=5*/s32[]{:T(128)}, s32[]{:T(128)}) while((s32[]{:T(128)}, f32[3,8,64,256]{3,2,1,0:T(8,128)S(1)}, s32[16]{0:T(128)}, bf16[20,3,8,64,256]{4,3,2,1,0:T(8,128)(2,1)}, s32[]{:T(128)}, ...), condition=%wide.region_3.0_spmd.clone, body=%wide.region_2.3_spmd.clone.sunk | while | flops 1179654 | bytes 3932305 | solution.py:120
  10.4 1.7 convert_add_fusion.2
  15.3 1.7 convert_add_fusion.2
  20.1 1.7 convert_add_fusion.2
  25.0 1.7 convert_add_fusion.2
  29.8 1.7 convert_add_fusion.2
  34.7 1.7 convert_add_fusion.2
  39.5 1.7 convert_add_fusion.2
  44.4 1.7 convert_add_fusion.2
  49.2 1.7 convert_add_fusion.2
  54.1 1.7 convert_add_fusion.2
  58.9 1.7 convert_add_fusion.2
  63.8 1.7 convert_add_fusion.2
  68.6 1.7 convert_add_fusion.2
  73.5 1.7 convert_add_fusion.2
  78.3 1.7 convert_add_fusion.2
  83.2 1.7 convert_add_fusion.2
  85.5 69.6 %while.29 = (s32[]{:T(128)}, f32[6,64,256]{2,1,0:T(8,128)S(1)}, s32[16]{0:T(128)S(1)}, bf16[20,3,8,64,256]{4,3,2,1,0:T(8,128)(2,1)}, f32[3,8,64,256]{3,2,1,0:T(8,128)S(1)}, /*index=5*/s32[]{:T(128)}, s32[]{:T(128)}, s32[]{:T(128)}) while((s32[]{:T(128)}, f32[6,64,256]{2,1,0:T(8,128)S(1)}, s32[16]{0:T(128)S(1)}, ...), condition=%wide.region_11.12_spmd.clone, body=%wide.region_4.11_spmd.clone.sunk | while | flops 2457606 | bytes 7864473 | solution.py:127
  88.0 1.4 convert_subtract_fusion.2
  92.4 1.4 convert_subtract_fusion.2
  96.7 1.4 convert_subtract_fusion.2
  101.1 1.4 convert_subtract_fusion.2
  105.4 1.4 convert_subtract_fusion.2
  109.8 1.4 convert_subtract_fusion.2
  114.1 1.4 convert_subtract_fusion.2
  118.5 1.4 convert_subtract_fusion.2
  122.8 1.4 convert_subtract_fusion.2
  127.2 1.4 convert_subtract_fusion.2
  131.5 1.4 convert_subtract_fusion.2
  155.9 1.7 fusion.64
  158.9 5.6 %collective-permute-start.4 = (f32[5,8,1,256]{3,2,1,0:T(1,128)S(1)}, f32[5,8,1,256]{3,2,1,0:T(1,128)S(1)}, u32[]{:S(2)}, u32[]{:S(2)}) collective-permute-start(f32[5,8,1,256]{3,2,1,0:T(1,128)S(1)} %get-tuple-element.251), channel_id=1, source_target_pairs={{0,1},{1,2},{2,3},{4,5},{5,6},{6,7},{8,9},{9,10},{10,11},{12,13},{... | collective-permute-start | bytes 122888 | tf_op jit(solution)/shard_map/ppermute | solution.py:21
  164.5 2.0 fusion.63
  166.5 2.9 %collective-permute-start.1 = (f32[5,1,64,256]{3,2,1,0:T(8,128)}, f32[5,1,64,256]{3,2,1,0:T(8,128)}, u32[]{:S(2)}, u32[]{:S(2)}) collective-permute-start(f32[5,1,64,256]{3,2,1,0:T(8,128)} %get-tuple-element.248), channel_id=1, source_target_pairs={{4,0},{8,4},{12,8},{0,12},{5,1},{9,5},{13,9},{1,13},{6,2},{10,6},{... | collective-permute-start | bytes 983048 | tf_op jit(solution)/shard_map/ppermute | solution.py:24
  170.2 26.6 %all-gather.3.cloned.1.call-done = f32[24,64,256]{2,1,0:T(8,128)} async-done(((f32[6,64,256]{2,1,0:T(8,128)}), f32[24,64,256]{2,1,0:T(8,128)}) %all-gather.3.cloned.1.call-update) | async-done | bytes 1572880 | tf_op jit(solution)/shard_map/all_gather | solution.py:133
  196.8 1.6 reduce_sum.116
  198.5 1.6 collective-permute-done
  201.5 4.1 %all-to-all-start = ((f32[4,2,6,2048]{3,1,2,0:T(2,128)}), f32[4,2,6,2048]{3,1,2,0:T(2,128)S(1)}, u32[]{:S(2)}, u32[]{:S(2)}) async-start(f32[4,2,6,2048]{3,1,2,0:T(2,128)} %fusion.48), calls=%async_computation | async-start | bytes 786432 | tf_op jit(solution)/shard_map/all_to_all | solution.py:89
  205.8 3.2 %fusion.65 = (f32[5,8,64,1]{3,2,1,0:T(8,128)S(1)}, f32[5,8,64,1]{3,2,1,0:T(8,128)}) fusion(f32[5,8,64,256]{3,2,1,0:T(8,128)} %bitcast.78), kind=kLoop, calls=%fused_computation.139 | loop fusion | bytes 40960 | tf_op jit(solution)/shard_map/slice | solution.py:47
  209.0 8.6 %all-to-all-done = f32[4,2,6,2048]{3,1,2,0:T(2,128)S(1)} async-done(((f32[4,2,6,2048]{3,1,2,0:T(2,128)}), f32[4,2,6,2048]{3,1,2,0:T(2,128)S(1)}, u32[]{:S(2)}, u32[]{:S(2)}) %all-to-all-start) | async-done | bytes 393248 | tf_op jit(solution)/shard_map/all_to_all | solution.py:89
  221.4 2.0 fusion.62
  223.6 7.1 %broadcast_multiply_fusion = (f32[5,8,64,256]{3,2,1,0:T(8,128)S(1)}, f32[5,8,64,256]{3,2,1,0:T(8,128)S(1)}) fusion(f32[8,64,256]{2,1,0:T(8,128)} %copy-done.6, f32[5,8,64,256]{3,2,1,0:T(8,128)S(1)} %bitcast.79, f32[1,8,64,256]{3,2,1,0:T(8,128)S(1)} %get-tuple-element.254, f32[3,8,64,256]{3,2,1,0:T(8,128)S(1)} %broadcast_in_dim.13, f32[5]{0:T(128)S(1)} %pad.16.clone, ...), kind=kLoop, calls=%fused_computation.65 | loop fusion | flops 17694720 | bytes 14410004 | tf_op jit(solution)/shard_map/mul | solution.py:57
  231.8 2.3 fusion.61
  234.1 1.5 collective-permute-start.5
  237.5 4.5 %collective-permute-start.8 = (f32[5,8,1,256]{3,2,1,0:T(1,128)S(1)}, f32[5,8,1,256]{3,2,1,0:T(1,128)S(1)}, u32[]{:S(2)}, u32[]{:S(2)}) collective-permute-start(f32[5,8,1,256]{3,2,1,0:T(1,128)S(1)} %get-tuple-element.243), channel_id=1, source_target_pairs={{0,1},{1,2},{2,3},{4,5},{5,6},{6,7},{8,9},{9,10},{10,11},{12,13},{... | collective-permute-start | bytes 122888 | tf_op jit(solution)/shard_map/ppermute | solution.py:21
  242.1 2.0 fusion.58
  244.1 1.8 broadcast_in_dim_reshape.3
  245.9 5.2 %collective-permute-done.6 = f32[5,1,64,256]{3,2,1,0:T(8,128)} collective-permute-done((f32[5,1,64,256]{3,2,1,0:T(8,128)}, f32[5,1,64,256]{3,2,1,0:T(8,128)}, u32[]{:S(2)}, u32[]{:S(2)}) %collective-permute-start.6) | collective-permute-done | bytes 327712 | tf_op jit(solution)/shard_map/ppermute | solution.py:21
  251.1 14.8 %fusion.9 = f32[1,5,8,64,256]{4,3,2,1,0:T(8,128)} fusion(f32[5,8,64,256]{3,2,1,0:T(8,128)} %copy-done.3, f32[5,8,64,1]{3,2,1,0:T(8,128)} %get-tuple-element.245, f32[5,8,64,1]{3,2,1,0:T(8,128)} %get-tuple-element.244, f32[5,8,1,256]{3,2,1,0:T(1,128)S(1)} %collective-permute-done.8, f32[5,8,1,256]{3,2,1,0:T(1,128)S(1)} %collective-permute-done.7, ...), kind=kLoop, calls=%fused_computation.25 | loop fusion | flops 18350080 | bytes 13885716 | tf_op jit(solution)/shard_map/broadcast_in_dim | solution.py:171
  (241 shorter events, 54.5 us)
Async XLA Ops:
  7.2 162.7 %copy-start = (s32[1,32]{1,0:T(1,128)S(1)}, s32[1,32]{1,0:T(1,128)}, u32[]{:S(2)}) copy-start(s32[1,32]{1,0:T(1,128)} %param.15) | copy-start | bytes 388
  7.2 189.6 %all-gather.3.cloned.1.call-start = ((), (), s32[]{:S(2)}) async-start(), calls=%async_computation.1 | async-start | bytes 1966080 | tf_op jit(solution)/shard_map/all_gather | solution.py:133
  84.8 0.7 copy-start.10
  155.1 14.3 %copy-start.9 = (s32[1,32]{1,0:T(1,128)S(1)}, s32[1,32]{1,0:T(1,128)}, u32[]{:S(2)}) copy-start(s32[1,32]{1,0:T(1,128)} %param.14) | copy-start | bytes 388
  157.6 65.7 %collective-permute-start.3 = (f32[5,8,1,256]{3,2,1,0:T(1,128)}, f32[5,8,1,256]{3,2,1,0:T(1,128)S(1)}, u32[]{:S(2)}, u32[]{:S(2)}) collective-permute-start(f32[5,8,1,256]{3,2,1,0:T(1,128)} %get-tuple-element.250), channel_id=1, source_target_pairs={{1,0},{2,1},{3,2},{5,4},{6,5},{7,6},{9,8},{10,9},{11,10},{13,12},{... | collective-permute-start | bytes 122888 | tf_op jit(solution)/shard_map/ppermute | solution.py:24
  158.9 64.5 %collective-permute-start.4 = (f32[5,8,1,256]{3,2,1,0:T(1,128)S(1)}, f32[5,8,1,256]{3,2,1,0:T(1,128)S(1)}, u32[]{:S(2)}, u32[]{:S(2)}) collective-permute-start(f32[5,8,1,256]{3,2,1,0:T(1,128)S(1)} %get-tuple-element.251), channel_id=1, source_target_pairs={{0,1},{1,2},{2,3},{4,5},{5,6},{6,7},{8,9},{9,10},{10,11},{12,13},{... | collective-permute-start | bytes 122888 | tf_op jit(solution)/shard_map/ppermute | solution.py:21
  166.5 56.9 %collective-permute-start.1 = (f32[5,1,64,256]{3,2,1,0:T(8,128)}, f32[5,1,64,256]{3,2,1,0:T(8,128)}, u32[]{:S(2)}, u32[]{:S(2)}) collective-permute-start(f32[5,1,64,256]{3,2,1,0:T(8,128)} %get-tuple-element.248), channel_id=1, source_target_pairs={{4,0},{8,4},{12,8},{0,12},{5,1},{9,5},{13,9},{1,13},{6,2},{10,6},{... | collective-permute-start | bytes 983048 | tf_op jit(solution)/shard_map/ppermute | solution.py:24
  169.4 54.0 %collective-permute-start.2 = (f32[5,1,64,256]{3,2,1,0:T(8,128)}, f32[5,1,64,256]{3,2,1,0:T(8,128)}, u32[]{:S(2)}, u32[]{:S(2)}) collective-permute-start(f32[5,1,64,256]{3,2,1,0:T(8,128)} %get-tuple-element.249), channel_id=1, source_target_pairs={{0,4},{4,8},{8,12},{12,0},{1,5},{5,9},{9,13},{13,1},{2,6},{6,10},{... | collective-permute-start | bytes 983048 | tf_op jit(solution)/shard_map/ppermute | solution.py:21
  198.4 1.8 collective-permute-start
  201.5 16.1 %all-to-all-start = ((f32[4,2,6,2048]{3,1,2,0:T(2,128)}), f32[4,2,6,2048]{3,1,2,0:T(2,128)S(1)}, u32[]{:S(2)}, u32[]{:S(2)}) async-start(f32[4,2,6,2048]{3,1,2,0:T(2,128)} %fusion.48), calls=%async_computation | async-start | bytes 786432 | tf_op jit(solution)/shard_map/all_to_all | solution.py:89
  218.2 0.7 copy-start.7
  219.1 1.9 copy-start.1
  219.8 1.6 copy-start.6
  221.4 2.2 copy-start.8
  223.6 7.2 %copy-start.5 = (f32[3,8,64,256]{3,2,1,0:T(8,128)}, f32[3,8,64,256]{3,2,1,0:T(8,128)S(1)}, u32[]{:S(2)}) copy-start(f32[3,8,64,256]{3,2,1,0:T(8,128)S(1)} %broadcast_in_dim.13) | copy-start | bytes 4718596
  230.8 5.4 %copy-start.3 = (f32[5,8,64,256]{3,2,1,0:T(8,128)}, f32[5,8,64,256]{3,2,1,0:T(8,128)S(1)}, u32[]{:S(2)}) copy-start(f32[5,8,64,256]{3,2,1,0:T(8,128)S(1)} %get-tuple-element.235) | copy-start | bytes 7864324
  230.8 11.3 %copy-start.4 = (f32[5,8,64,256]{3,2,1,0:T(8,128)}, f32[5,8,64,256]{3,2,1,0:T(8,128)S(1)}, u32[]{:S(2)}) copy-start(f32[5,8,64,256]{3,2,1,0:T(8,128)S(1)} %get-tuple-element.234) | copy-start | bytes 7864324
  234.1 11.8 %collective-permute-start.5 = (f32[5,1,64,256]{3,2,1,0:T(8,128)}, f32[5,1,64,256]{3,2,1,0:T(8,128)}, u32[]{:S(2)}, u32[]{:S(2)}) collective-permute-start(f32[5,1,64,256]{3,2,1,0:T(8,128)} %get-tuple-element.240), channel_id=1, source_target_pairs={{4,0},{8,4},{12,8},{0,12},{5,1},{9,5},{13,9},{1,13},{6,2},{10,6},{... | collective-permute-start | bytes 983048 | tf_op jit(solution)/shard_map/ppermute | solution.py:24
  235.6 15.5 %collective-permute-start.6 = (f32[5,1,64,256]{3,2,1,0:T(8,128)}, f32[5,1,64,256]{3,2,1,0:T(8,128)}, u32[]{:S(2)}, u32[]{:S(2)}) collective-permute-start(f32[5,1,64,256]{3,2,1,0:T(8,128)} %get-tuple-element.241), channel_id=1, source_target_pairs={{0,4},{4,8},{8,12},{12,0},{1,5},{5,9},{9,13},{13,1},{2,6},{6,10},{... | collective-permute-start | bytes 983048 | tf_op jit(solution)/shard_map/ppermute | solution.py:21
  236.2 9.7 %collective-permute-start.7 = (f32[5,8,1,256]{3,2,1,0:T(1,128)S(1)}, f32[5,8,1,256]{3,2,1,0:T(1,128)S(1)}, u32[]{:S(2)}, u32[]{:S(2)}) collective-permute-start(f32[5,8,1,256]{3,2,1,0:T(1,128)S(1)} %get-tuple-element.242), channel_id=1, source_target_pairs={{1,0},{2,1},{3,2},{5,4},{6,5},{7,6},{9,8},{10,9},{11,10},{13,12},{... | collective-permute-start | bytes 122888 | tf_op jit(solution)/shard_map/ppermute | solution.py:24
  237.5 8.4 %collective-permute-start.8 = (f32[5,8,1,256]{3,2,1,0:T(1,128)S(1)}, f32[5,8,1,256]{3,2,1,0:T(1,128)S(1)}, u32[]{:S(2)}, u32[]{:S(2)}) collective-permute-start(f32[5,8,1,256]{3,2,1,0:T(1,128)S(1)} %get-tuple-element.243), channel_id=1, source_target_pairs={{0,1},{1,2},{2,3},{4,5},{5,6},{6,7},{8,9},{9,10},{10,11},{12,13},{... | collective-permute-start | bytes 122888 | tf_op jit(solution)/shard_map/ppermute | solution.py:21
  242.1 9.0 %copy-start.2 = (f32[1,5,8,64,256]{4,3,2,1,0:T(8,128)S(1)}, f32[1,5,8,64,256]{4,3,2,1,0:T(8,128)}, u32[]{:S(2)}) copy-start(f32[1,5,8,64,256]{4,3,2,1,0:T(8,128)} %param.12) | copy-start | bytes 7864324
Sparse Core Ops, SparseCore 0:
  156.0 40.7 all-gather.2
